TPU v7x, 32 devices: a whole 2x2x4 slice. The times are simulated.
32 devices in a mesh: gx: 4 (over y, core), gy: 8 (over z, x).
Axes of the slice: x: 2, y: 2, z: 4, core: 2. Of those that a mesh axis runs over, the one named last changes fastest.
Arguments:
- right_side: float32 [64, 256, 128], P('gx', 'gy'), may hold values from -6 to 6
- first_guess: float32 [64, 256, 128], P('gx', 'gy'), may hold values from -6 to 6
- recycled: bfloat16 [8, 64, 256, 128], P(None, 'gx', 'gy'), may hold values from -4 to 4
- heights: int32 [64, 256], P('gx', 'gy'), may hold values from 0 to 64, as said below
- ground_codes: int32 [64, 256], P('gx', 'gy'), may hold values from 0 to 2
Outputs:
- solution: float32 [64, 256, 128], P('gx', 'gy')
- residual: float32 [64, 256, 128], P('gx', 'gy')
Inputs may be any that keep to these rules, and one draw needn't show every extreme that they name: `heights`: height of the buildings standing in each column, 0 for open ground.
All inputs are finite; a program needn't handle non-finite values.
Results may differ from a plain program's by a relative error of at most 0.0003.
Values sent between devices are 32-bit elements; how exact they have to be, the bound alone decides.
A program may use at most 64 MiB of HBM per device.

v0:
```python
import functools

import jax
import jax.numpy as jnp
from jax import lax
from jax.experimental import pallas as pl
from jax.experimental.pallas import tpu as pltpu
from jax.sharding import PartitionSpec as P

OUTER = 2
SWEEPS = 3
GHOST = SWEEPS

CENTER = 7.25
HALF = 6.75
SIGMA = 7.25 / 6.75

F32 = jnp.float32


def kernel(
    gxn, gyn, count, a, b,
    rs_hbm, fg_hbm, rec_hbm, h_hbm, code_hbm,
    sol_ref, res_ref,
    rs_ref, fg_ref, rec_ref, ground, near_ground,
    wide0, xsend0, ysend0, yrecv0, rwide, ysend, yrecv, csend, crecv,
    fwide, diag, uwide, dwide, rem, cbuf, img, psend, slots,
    in_sem, gs_sem, gr_sem, hs_sem, hr_sem, ds_sem, dr_sem, ps_sem, pr_sem,
):
    lanes = 128
    S = b + 16
    n = gxn * gyn
    nf = count + 1
    gx = lax.axis_index("gx")
    gy = lax.axis_index("gy")
    me = gx * gyn + gy

    def at_dev(i, j):
        return dict(device_id={"gx": i, "gy": j}, device_id_type=pl.DeviceIdType.MESH)

    loads = [
        pltpu.make_async_copy(h_hbm, ground.at[0], in_sem.at[0]),
        pltpu.make_async_copy(code_hbm, ground.at[1], in_sem.at[1]),
        pltpu.make_async_copy(fg_hbm, fg_ref, in_sem.at[2]),
        pltpu.make_async_copy(rs_hbm, rs_ref, in_sem.at[3]),
    ] + [pltpu.make_async_copy(rec_hbm.at[m], rec_ref.at[m], in_sem.at[4 + m]) for m in range(count)]
    for cp in loads:
        cp.start()

    barrier = pltpu.get_barrier_semaphore()

    def greet(t, _):
        peer = lax.rem(me + t, n)
        pl.semaphore_signal(barrier, inc=1, **at_dev(peer // gyn, lax.rem(peer, gyn)))
        return 0

    lax.fori_loop(1, n, greet, 0)

    def base0(x):
        return S * (x + 1) + 8

    def base(x):
        return S * (x + GHOST) + 8

    def span(x):
        return pl.ds(S * (x + GHOST), S)

    lane8 = lax.broadcasted_iota(jnp.int32, (8, lanes), 1)
    sub8 = lax.broadcasted_iota(jnp.int32, (8, lanes), 0)
    row1 = lax.broadcasted_iota(jnp.int32, (1, lanes), 1)

    steps = ((-1, 0), (1, 0), (0, -1), (0, 1), (-1, -1), (-1, 1), (1, -1), (1, 1))
    opposite = [steps.index((-i, -j)) for i, j in steps]
    have, peers = [], []
    for i, j in steps:
        ok = None
        for at, size, by in ((gx, gxn, i), (gy, gyn, j)):
            if by:
                one = at > 0 if by < 0 else at < size - 1
                ok = one if ok is None else jnp.logical_and(ok, one)
        have.append(ok)
        peers.append(at_dev(gx + i, gy + j))

    def ground_copy(s):
        return pltpu.make_async_remote_copy(
            src_ref=ground, dst_ref=near_ground.at[opposite[s]],
            send_sem=gs_sem.at[s], recv_sem=gr_sem.at[opposite[s]], **peers[s],
        )

    def field_copy(m, s):
        w = wide0.at[m]
        src = (
            xsend0.at[m, 0], xsend0.at[m, 1],
            ysend0.at[m, 0], ysend0.at[m, 1],
        )[s]
        dst = (
            w.at[pl.ds(base0(a), b), :], w.at[pl.ds(base0(-1), b), :],
            yrecv0.at[m, 1], yrecv0.at[m, 0],
        )[s]
        return pltpu.make_async_remote_copy(
            src_ref=src, dst_ref=dst,
            send_sem=hs_sem.at[m, s], recv_sem=hr_sem.at[m, opposite[s]], **peers[s],
        )

    def deep_copies(r, s):
        w = rwide.at[r]
        if s < 2:
            pieces = [
                (
                    w.at[pl.ds(base(i if s == 0 else a - GHOST + i), b), :],
                    w.at[pl.ds(base(a + i if s == 0 else i - GHOST), b), :],
                )
                for i in range(GHOST)
            ]
        elif s < 4:
            pieces = [(ysend.at[r, s - 2], yrecv.at[r, 3 - s])]
        else:
            pieces = [(csend.at[r, s - 4], crecv.at[r, opposite[s] - 4])]
        return [
            pltpu.make_async_remote_copy(
                src_ref=p, dst_ref=q,
                send_sem=ds_sem.at[r, s, i], recv_sem=dr_sem.at[r, opposite[s], i], **peers[s],
            )
            for i, (p, q) in enumerate(pieces)
        ]

    def each(sides, act):
        for s in sides:
            @pl.when(have[s])
            def _(s=s):
                act(s)

    def all_do(cps, what):
        for cp in cps:
            getattr(cp, what)()

    zeros = jnp.zeros((b, lanes), F32)
    for s in range(8):
        @pl.when(jnp.logical_not(have[s]))
        def _(s=s):
            near_ground[s, 0] = jnp.full((a, b), 255, jnp.int32)
            near_ground[s, 1] = jnp.zeros((a, b), jnp.int32)
            if s < 2:
                for m in range(nf):
                    wide0[m, pl.ds(base0(-1 if s == 0 else a), b), :] = zeros
                for r in range(OUTER):
                    for i in range(GHOST):
                        rwide[r, pl.ds(base(i - GHOST if s == 0 else a + i), b), :] = zeros
            elif s < 4:
                for m in range(nf):
                    yrecv0[m, s - 2] = jnp.zeros((a, lanes), F32)
                for r in range(OUTER):
                    for i in range(GHOST):
                        yrecv[r, s - 2, i] = jnp.zeros((a, lanes), F32)
            else:
                for r in range(OUTER):
                    for i in range(3):
                        crecv[r, s - 4, i] = jnp.zeros((1, lanes), F32)

    ones = jnp.ones((b, lanes), jnp.bfloat16)
    yi = lax.broadcasted_iota(jnp.int32, (S, b), 0)
    ji = lax.broadcasted_iota(jnp.int32, (S, b), 1)
    lane_f = lax.broadcasted_iota(jnp.int32, (S, lanes), 1).astype(F32)
    lane_s = lax.broadcasted_iota(jnp.int32, (S, lanes), 1)

    def spread(tables, i):
        left, mid, right = [jnp.broadcast_to(t[i : i + 1, :].astype(F32), (S, b)) for t in tables]
        pick = jnp.where(yi - 8 == ji, mid, 0.0)
        pick = jnp.where(yi == ji - (b - 8), left, pick)
        pick = jnp.where(yi - (b + 8) == ji, right, pick)
        return jnp.dot(pick.astype(jnp.bfloat16), ones, preferred_element_type=F32)

    def mask_row(x, trio, i):
        high = spread([t.at[0] for t in trio], i)
        code = spread([t.at[1] for t in trio], i)
        fwide[span(x), :] = jnp.where(lane_f >= high, 1.0, 0.0)
        bottom = jnp.where(code == 1.0, 0.5, 0.0) + jnp.where(code == 2.0, 2.0, 0.0)
        diag[span(x), :] = jnp.where(lane_s == 0, bottom, 0.0) + jnp.where(
            lane_s == lanes - 1, 1.0, 0.0
        )

    def fluid(x):
        return fwide[pl.ds(base(x), b), :]

    def prepare(m):
        loads[2 if m == count else 4 + m].wait()
        w = wide0.at[m]
        for x in range(a):
            rows = slice(x * b, x * b + b)
            v = fg_ref[rows, :] if m == count else rec_ref[m, rows, :].astype(F32)
            w[pl.ds(base0(x), b), :] = v
            if x == 0:
                xsend0[m, 0] = v
            if x == a - 1:
                xsend0[m, 1] = v
        ysend0[m, 0] = w[pl.ds(S + 8, a, stride=S), :]
        ysend0[m, 1] = w[pl.ds(S + 8 + b - 1, a, stride=S), :]

    order = [count] + list(range(count))
    early = order[: (nf + 1) // 2]
    for m in early:
        prepare(m)
    all_do(loads[:2], "wait")
    pl.semaphore_wait(barrier, n - 1)
    each((4, 5, 6, 7, 2, 3, 0, 1), lambda s: ground_copy(s).start())
    for m in early:
        each((2, 3, 0, 1), lambda s: field_copy(m, s).start())
    for m in order[len(early) :]:
        prepare(m)
        each((2, 3, 0, 1), lambda s: field_copy(m, s).start())

    for x in range(a):
        mask_row(x, (ground,) * 3, x)

    @pl.loop(0, nf)
    def _(m):
        for x in range(a):
            at = pl.ds(base0(x), b)
            wide0[m, at, :] = fluid(x) * wide0[m, at, :]

    each(range(8), lambda s: ground_copy(opposite[s]).wait_recv())
    for x in range(-GHOST, a + GHOST):
        if x < 0:
            trio, i = (near_ground.at[4], near_ground.at[0], near_ground.at[5]), a + x
        elif x < a:
            trio, i = (near_ground.at[2], ground, near_ground.at[3]), x
        else:
            trio, i = (near_ground.at[6], near_ground.at[1], near_ground.at[7]), x - a
        mask_row(x, trio, i)

    def near(w, at, size):
        c = w[pl.ds(at, size), :]
        lane = lax.broadcasted_iota(jnp.int32, (size, lanes), 1)
        up = jnp.where(lane == lanes - 1, 0.0, pltpu.roll(c, lanes - 1, 1))
        down = jnp.where(lane == 0, 0.0, pltpu.roll(c, 1, 1))
        return (
            (w[pl.ds(at + S, size), :] + w[pl.ds(at - S, size), :])
            + (w[pl.ds(at + 1, size), :] + w[pl.ds(at - 1, size), :])
            + (up + down)
        )

    for x in range(1 - GHOST, a + GHOST - 1):
        f = fwide[span(x), :]
        diag[span(x), :] = f * (near(fwide, S * (x + GHOST), S) + diag[span(x), :]) + (1.0 - f)

    def arrive(m):
        each(range(4), lambda s: field_copy(m, opposite[s]).wait_recv())
        w = wide0.at[m]
        for x in (-1, a):
            at = pl.ds(base0(x), b)
            w[at, :] = fluid(x) * w[at, :]
        for i, x in enumerate((-1, b)):
            w[pl.ds(base0(0) + x, a, stride=S), :] = (
                fwide[pl.ds(base(0) + x, a, stride=S), :] * yrecv0[m, i]
            )

    def total(v):
        out = v[0:8]
        for i in range(8, b, 8):
            out = out + v[i : i + 8]
        return out

    zero8 = jnp.zeros((8, lanes), F32)
    table = {}
    loads[3].wait()
    for m in order:
        arrive(m)
        sums = [zero8] * (m + 2)
        for x in range(a):
            rows = slice(x * b, x * b + b)
            dg = diag[pl.ds(base(x), b), :]
            flow = fluid(x) * near(wide0.at[m], base0(x), b)
            if m == count:
                res_ref[rows, :] = rs_ref[rows, :] - (dg * fg_ref[rows, :] - flow)
                continue
            v = dg * rec_ref[m, rows, :].astype(F32) - flow
            img[m, rows, :] = v
            others = [img[q, rows, :] for q in range(m)] + [v, res_ref[rows, :]]
            sums = [acc + total(v * o) for acc, o in zip(sums, others)]
        if m < count:
            for q in range(m + 1):
                table[(q, m)] = sums[q]
            table[m] = sums[m + 1]

    def column(items):
        rows = [jnp.sum(v, axis=0, keepdims=True) for v in items]
        if len(rows) < 8:
            rows.append(jnp.zeros((8 - len(rows), lanes), F32))
        return jnp.sum(jnp.concatenate(rows, axis=0), axis=1, keepdims=True)

    packed = zero8
    for q in range(count + 1):
        items = (
            [table[(min(m, q), max(m, q))] for m in range(count)]
            if q < count
            else [table[m] for m in range(count)]
        )
        packed = packed + jnp.where(lane8 == 16 * sub8 + q, column(items), 0.0)

    def all_sum(k, row):
        psend[k] = row
        slots[k, me] = row

        def send(t, _):
            peer = lax.rem(me + t, n)
            pltpu.make_async_remote_copy(
                src_ref=psend.at[k], dst_ref=slots.at[k, me],
                send_sem=ps_sem.at[k], recv_sem=pr_sem.at[k],
                **at_dev(peer // gyn, lax.rem(peer, gyn)),
            ).start()
            return 0

        lax.fori_loop(1, n, send, 0)
        most = slots.at[k, pl.ds(0, n - 1)]
        pltpu.make_async_copy(most, most, pr_sem.at[k]).wait()
        out = jnp.sum(slots[k], axis=0)
        return out

    row = all_sum(0, jnp.sum(packed, axis=0, keepdims=True))

    wrow = jnp.broadcast_to(row, (8, lanes))
    mat = zero8
    for m in range(count):
        moved = wrow if m == 0 else pltpu.roll(wrow, lanes - 16 * m, 1)
        mat = jnp.where(sub8 == m, moved, mat)
    mat = jnp.where(lane8 <= count, mat, 0.0) + jnp.where(lane8 == 16 + sub8, 1.0, 0.0)
    for k in range(count):
        pivot = mat[k : k + 1, :] / mat[k : k + 1, k : k + 1]
        mat = jnp.where(sub8 == k, pivot, mat - mat[:, k : k + 1] * pivot)
    inverse = pltpu.roll(mat, lanes - 16, 1)

    def whole(v):
        return jnp.concatenate([jnp.broadcast_to(v, (8, lanes))] * (b // 8), axis=0)

    coeffs = [whole(mat[m : m + 1, count : count + 1]) for m in range(count)]

    def first_update(x, _):
        rows = pl.ds(pl.multiple_of(x * b, 8), b)
        res = res_ref[rows, :]
        for m in range(count):
            res = res - coeffs[m] * img[m, rows, :]
        rwide[0, pl.ds(pl.multiple_of(base(x), 8), b), :] = res
        return 0

    lax.fori_loop(0, a, first_update, 0)

    def first_solution(x, _):
        rows = pl.ds(pl.multiple_of(x * b, 8), b)
        sol = fg_ref[rows, :]
        for m in range(count):
            sol = sol + coeffs[m] * rec_ref[m, rows, :].astype(F32)
        sol_ref[rows, :] = sol
        return 0

    later = first_solution

    bits = ((0, 0), (0, 1), (1, 0))

    for outer in range(OUTER):
        w = rwide.at[outer]
        for i in range(GHOST):
            ysend[outer, 0, i] = w[pl.ds(base(0) + i, a, stride=S), :]
            ysend[outer, 1, i] = w[pl.ds(base(0) + b - 1 - i, a, stride=S), :]
        for s in range(4, 8):
            for i, (p, q) in enumerate(bits):
                x = p if steps[s][0] < 0 else a - 1 - p
                y = q if steps[s][1] < 0 else b - 1 - q
                csend[outer, s - 4, i] = w[pl.ds(base(x) + y, 1), :]
        each((4, 5, 6, 7, 2, 3, 0, 1), lambda s: all_do(deep_copies(outer, s), "start"))
        lax.fori_loop(0, a, later, 0)

        def dots_residual(i, accs):
            x, y = i // (b // 8), lax.rem(i, b // 8)
            at = pl.multiple_of(i * 8, 8)
            res = w[pl.ds(pl.multiple_of(base(x) + y * 8, 8), 8), :]
            return tuple(acc + img[m, pl.ds(at, 8), :] * res for m, acc in enumerate(accs))

        alongs = column(lax.fori_loop(0, a * b // 8, dots_residual, (zero8,) * count))
        each(range(8), lambda s: all_do(deep_copies(outer, opposite[s]), "wait_recv"))
        for i in range(GHOST):
            w[pl.ds(base(0) - 1 - i, a, stride=S), :] = yrecv[outer, 0, i]
            w[pl.ds(base(0) + b + i, a, stride=S), :] = yrecv[outer, 1, i]
        for s in range(4, 8):
            for i, (p, q) in enumerate(bits):
                x = -1 - p if steps[s][0] < 0 else a + p
                y = -1 - q if steps[s][1] < 0 else b + q
                w[pl.ds(base(x) + y, 1), :] = crecv[outer, s - 4, i]
        for x in range(-GHOST, a + GHOST):
            uwide[0, span(x), :] = fwide[span(x), :] * (w[span(x), :] * (1.0 / CENTER))
        rho = 1.0 / SIGMA
        for sweep in range(SWEEPS):
            rho_new = 1.0 / (2.0 * SIGMA - rho)
            grow = SWEEPS - 1 - sweep
            for x in range(-grow, a + grow):
                at, size = (base(x), b) if grow == 0 else (S * (x + GHOST), S)
                rows = pl.ds(at, size)
                f = fwide[rows, :]
                old = w[rows, :] if sweep == 0 else rem[rows, :]
                d = old * (1.0 / CENTER) if sweep == 0 else dwide[rows, :]
                left = old - (diag[rows, :] * d - f * near(uwide.at[sweep], at, size))
                cbuf[rows, :] = d if sweep == 0 else cbuf[rows, :] + d
                rem[rows, :] = left
                if sweep + 1 < SWEEPS:
                    d = (rho_new * rho) * d + (2.0 * rho_new / HALF) * left
                    dwide[rows, :] = d
                    uwide[sweep + 1, rows, :] = f * d
            rho = rho_new

        def dots(i, accs):
            x, y = i // (b // 8), lax.rem(i, b // 8)
            at = pl.multiple_of(i * 8, 8)
            wat = pl.multiple_of(base(x) + y * 8, 8)
            res = rwide[outer, pl.ds(wat, 8), :]
            w = res - rem[pl.ds(wat, 8), :]
            new = []
            for m in range(count):
                im = img[m, pl.ds(at, 8), :]
                new.append(accs[m] + im * w)
            new.append(accs[count] + w * res)
            new.append(accs[count + 1] + w * w)
            return tuple(new)

        accs = lax.fori_loop(0, a * b // 8, dots, (zero8,) * (count + 2))
        packed = (
            jnp.where(lane8 == sub8, column(accs[:count]), 0.0)
            + jnp.where(lane8 == sub8 + 8, alongs, 0.0)
            + jnp.where(lane8 == sub8 + 16, column(accs[count:]), 0.0)
        )
        row = all_sum(1 + outer, jnp.sum(packed, axis=0, keepdims=True))
        onto = jnp.sum(jnp.where(lane8 == sub8, jnp.broadcast_to(row, (8, lanes)), 0.0), axis=1, keepdims=True)
        y = jnp.sum(onto * inverse, axis=0, keepdims=True)
        y = jnp.where(row1 < count, y, 0.0)
        along = pltpu.roll(jnp.broadcast_to(row, (8, lanes)), lanes - 8, 1)[0:1]
        numerator = row[:, 16:17] - jnp.sum(y * along, axis=1, keepdims=True)
        denominator = row[:, 17:18] - jnp.sum(y * row, axis=1, keepdims=True)
        step = whole(numerator / denominator)
        ys = [whole(y[:, m : m + 1]) for m in range(count)]

        def update(x, _):
            rows = pl.ds(pl.multiple_of(x * b, 8), b)
            at = pl.ds(pl.multiple_of(base(x), 8), b)
            res = rwide[outer, at, :]
            w = res - rem[at, :]
            for m in range(count):
                w = w - ys[m] * img[m, rows, :]
            res = res - step * w
            if outer + 1 < OUTER:
                rwide[outer + 1, at, :] = res
            else:
                res_ref[rows, :] = res
            return 0

        lax.fori_loop(0, a, update, 0)

        def solution_update(x, _, step=step, ys=ys):
            rows = pl.ds(pl.multiple_of(x * b, 8), b)
            c = cbuf[pl.ds(pl.multiple_of(base(x), 8), b), :]
            for m in range(count):
                c = c - ys[m] * rec_ref[m, rows, :].astype(F32)
            sol_ref[rows, :] = sol_ref[rows, :] + step * c
            return 0

        later = solution_update

    lax.fori_loop(0, a, later, 0)

    for k in range(OUTER + 1):
        most = slots.at[k, pl.ds(0, n - 1)]
        pltpu.make_async_copy(most, most, ps_sem.at[k]).wait()
    each(range(8), lambda s: ground_copy(s).wait_send())
    for m in range(nf):
        each(range(4), lambda s: field_copy(m, s).wait_send())
    for r in range(OUTER):
        each(range(8), lambda s: all_do(deep_copies(r, s), "wait_send"))


def store(sol_ref, res_ref, sol_out, res_out, sem):
    cps = [
        pltpu.make_async_copy(sol_ref, sol_out, sem.at[0]),
        pltpu.make_async_copy(res_ref, res_out, sem.at[1]),
    ]
    for cp in cps:
        cp.start()
    for cp in cps:
        cp.wait()


def solution(mesh):
    gxn, gyn = mesh.shape["gx"], mesh.shape["gy"]

    def local(right_side, first_guess, recycled, heights, ground_codes):
        a, b, nz = right_side.shape
        count = recycled.shape[0]
        field = jax.ShapeDtypeStruct((a * b, nz), F32)
        vm = pl.BlockSpec(memory_space=pltpu.VMEM)
        wide_f = pltpu.VMEM(((a + 2 * GHOST) * (b + 16), nz), F32)
        n = gxn * gyn
        hbm = pl.BlockSpec(memory_space=pltpu.HBM)
        dma = pltpu.SemaphoreType.DMA
        sol, res = pl.pallas_call(
            functools.partial(kernel, gxn, gyn, count, a, b),
            out_shape=(field, field),
            in_specs=[hbm] * 5,
            out_specs=(vm, vm),
            scratch_shapes=[
                pltpu.VMEM((a * b, nz), F32),
                pltpu.VMEM((a * b, nz), F32),
                pltpu.VMEM((count, a * b, nz), jnp.bfloat16),
                pltpu.VMEM((2, a, b), jnp.int32),
                pltpu.VMEM((8, 2, a, b), jnp.int32),
                pltpu.VMEM((count + 1, (a + 2) * (b + 16), nz), F32),
                pltpu.VMEM((count + 1, 2, b, nz), F32),
                pltpu.VMEM((count + 1, 2, a, nz), F32),
                pltpu.VMEM((count + 1, 2, a, nz), F32),
                pltpu.VMEM((OUTER,) + wide_f.shape, F32),
                pltpu.VMEM((OUTER, 2, GHOST, a, nz), F32),
                pltpu.VMEM((OUTER, 2, GHOST, a, nz), F32),
                pltpu.VMEM((OUTER, 4, 3, 1, nz), F32),
                pltpu.VMEM((OUTER, 4, 3, 1, nz), F32),
                wide_f,
                wide_f,
                pltpu.VMEM((SWEEPS,) + wide_f.shape, F32),
                wide_f,
                wide_f,
                wide_f,
                pltpu.VMEM((count, a * b, nz), F32),
                pltpu.VMEM((OUTER + 1, 1, nz), F32),
                pltpu.VMEM((OUTER + 1, n, 1, nz), F32),
                dma((4 + count,)),
                dma((8,)),
                dma((8,)),
                dma((count + 1, 4)),
                dma((count + 1, 4)),
                dma((OUTER, 8, GHOST)),
                dma((OUTER, 8, GHOST)),
                dma((OUTER + 1,)),
                dma((OUTER + 1,)),
            ],
            compiler_params=pltpu.CompilerParams(
                collective_id=0, has_side_effects=True, vmem_limit_bytes=32 * 2**20
            ),
        )(*[
            pltpu.with_memory_space_constraint(v, pltpu.HBM)
            for v in (
                right_side.reshape(a * b, nz),
                first_guess.reshape(a * b, nz),
                recycled.reshape(count, a * b, nz),
                heights,
                ground_codes,
            )
        ])
        sol, res = pl.pallas_call(
            store,
            out_shape=(field, field),
            in_specs=[vm] * 2,
            out_specs=(hbm, hbm),
            scratch_shapes=[dma((2,))],
            compiler_params=pltpu.CompilerParams(vmem_limit_bytes=4 * 2**20),
        )(sol, res)
        return sol.reshape(a, b, nz), res.reshape(a, b, nz)

    placed = (
        P("gx", "gy", None),
        P("gx", "gy", None),
        P(None, "gx", "gy", None),
        P("gx", "gy"),
        P("gx", "gy"),
    )
    return jax.shard_map(
        local,
        mesh=mesh,
        in_specs=placed,
        out_specs=(P("gx", "gy", None), P("gx", "gy", None)),
        check_vma=False,
    )
```

profile of v0, /device:TPU:0, one launch (start us, length us, event | category | flops | bytes accessed | tf_op | source)
XLA Modules:
  0.0 44.9 jit_solution(6701986157786520768)
XLA Ops:
  0.6 43.5 %shard_map.68 = (f32[512,128]{1,0:T(8,128)S(1)}, f32[512,128]{1,0:T(8,128)S(1)}) custom-call(f32[512,128]{1,0:T(8,128)} %bitcast.6, f32[512,128]{1,0:T(8,128)} %bitcast.7, bf16[8,512,128]{2,1,0:T(8,128)(2,1)} %bitcast.5, s32[16,32]{1,0:T(8,128)} %h_hbm.1, s32[16,32]{1,0:T(8,128)} %code_hbm.1), custom_call_target="tpu_custom_call" | custom-call | tf_op jit(solution)/shard_map/pallas_call | solution.py:500
  44.1 0.8 %shard_map.69 = (f32[512,128]{1,0:T(8,128)}, f32[512,128]{1,0:T(8,128)}) custom-call(f32[512,128]{1,0:T(8,128)S(1)} %get-tuple-element.6.sol_ref, f32[512,128]{1,0:T(8,128)S(1)} %get-tuple-element.7.res_ref), custom_call_target="tpu_custom_call" | custom-call | tf_op jit(solution)/shard_map/pallas_call | solution.py:552
where the time goes:
time: 45.1 us; the launch traced here: 44.9 us
  Pallas kernels  44.3 us (98%)
  between operations  0.64 us (1%)
    pallas_call x1, Pallas kernels, local(): pl.pallas_call(functools.partial(kernel, gxn, gyn, count, a, b), out_shap...  43.5 us

commit v1 on v0

--- a/solution.py
+++ b/solution.py
@@ -297,20 +297,33 @@
         )
         packed = packed + jnp.where(lane8 == 16 * sub8 + q, column(items), 0.0)
 
+    gis = [lax.rem(gx + i, gxn) for i in range(gxn)]
+    gjs = [lax.rem(gy + j, gyn) for j in range(gyn)]
+    far_first = sorted(
+        [(i, j) for i in range(gxn) for j in range(gyn) if i or j],
+        key=lambda t: (abs(t[1] - gyn // 2), abs(t[0] - gxn // 2)),
+    )
+
     def all_sum(k, row):
         psend[k] = row
         slots[k, me] = row
 
-        def send(t, _):
-            peer = lax.rem(me + t, n)
+        def send(gi, gj):
             pltpu.make_async_remote_copy(
                 src_ref=psend.at[k], dst_ref=slots.at[k, me],
-                send_sem=ps_sem.at[k], recv_sem=pr_sem.at[k],
-                **at_dev(peer // gyn, lax.rem(peer, gyn)),
+                send_sem=ps_sem.at[k], recv_sem=pr_sem.at[k], **at_dev(gi, gj),
             ).start()
-            return 0
-
-        lax.fori_loop(1, n, send, 0)
+
+        if n <= 64:
+            for i, j in far_first:
+                send(gis[i], gjs[j])
+        else:
+            def step(t, _):
+                peer = lax.rem(me + t, n)
+                send(peer // gyn, lax.rem(peer, gyn))
+                return 0
+
+            lax.fori_loop(1, n, step, 0)
         most = slots.at[k, pl.ds(0, n - 1)]
         pltpu.make_async_copy(most, most, pr_sem.at[k]).wait()
         out = jnp.sum(slots[k], axis=0)
@@ -334,23 +347,19 @@
 
     coeffs = [whole(mat[m : m + 1, count : count + 1]) for m in range(count)]
 
-    def first_update(x, _):
-        rows = pl.ds(pl.multiple_of(x * b, 8), b)
+    for x in range(a):
+        rows = slice(x * b, x * b + b)
         res = res_ref[rows, :]
         for m in range(count):
             res = res - coeffs[m] * img[m, rows, :]
-        rwide[0, pl.ds(pl.multiple_of(base(x), 8), b), :] = res
-        return 0
-
-    lax.fori_loop(0, a, first_update, 0)
-
-    def first_solution(x, _):
-        rows = pl.ds(pl.multiple_of(x * b, 8), b)
+        rwide[0, pl.ds(base(x), b), :] = res
+
+    def first_solution(x):
+        rows = slice(x * b, x * b + b)
         sol = fg_ref[rows, :]
         for m in range(count):
             sol = sol + coeffs[m] * rec_ref[m, rows, :].astype(F32)
         sol_ref[rows, :] = sol
-        return 0
 
     later = first_solution
 
@@ -367,15 +376,15 @@
                 y = q if steps[s][1] < 0 else b - 1 - q
                 csend[outer, s - 4, i] = w[pl.ds(base(x) + y, 1), :]
         each((4, 5, 6, 7, 2, 3, 0, 1), lambda s: all_do(deep_copies(outer, s), "start"))
-        lax.fori_loop(0, a, later, 0)
-
-        def dots_residual(i, accs):
-            x, y = i // (b // 8), lax.rem(i, b // 8)
-            at = pl.multiple_of(i * 8, 8)
-            res = w[pl.ds(pl.multiple_of(base(x) + y * 8, 8), 8), :]
-            return tuple(acc + img[m, pl.ds(at, 8), :] * res for m, acc in enumerate(accs))
-
-        alongs = column(lax.fori_loop(0, a * b // 8, dots_residual, (zero8,) * count))
+        for x in range(a):
+            later(x)
+
+        accs = [zero8] * count
+        for x in range(a):
+            rows = slice(x * b, x * b + b)
+            res = w[pl.ds(base(x), b), :]
+            accs = [acc + total(img[m, rows, :] * res) for m, acc in enumerate(accs)]
+        alongs = column(accs)
         each(range(8), lambda s: all_do(deep_copies(outer, opposite[s]), "wait_recv"))
         for i in range(GHOST):
             w[pl.ds(base(0) - 1 - i, a, stride=S), :] = yrecv[outer, 0, i]
@@ -406,21 +415,14 @@
                     uwide[sweep + 1, rows, :] = f * d
             rho = rho_new
 
-        def dots(i, accs):
-            x, y = i // (b // 8), lax.rem(i, b // 8)
-            at = pl.multiple_of(i * 8, 8)
-            wat = pl.multiple_of(base(x) + y * 8, 8)
-            res = rwide[outer, pl.ds(wat, 8), :]
-            w = res - rem[pl.ds(wat, 8), :]
-            new = []
-            for m in range(count):
-                im = img[m, pl.ds(at, 8), :]
-                new.append(accs[m] + im * w)
-            new.append(accs[count] + w * res)
-            new.append(accs[count + 1] + w * w)
-            return tuple(new)
-
-        accs = lax.fori_loop(0, a * b // 8, dots, (zero8,) * (count + 2))
+        accs = [zero8] * (count + 2)
+        for x in range(a):
+            rows = slice(x * b, x * b + b)
+            at = pl.ds(base(x), b)
+            res = rwide[outer, at, :]
+            image = res - rem[at, :]
+            others = [img[m, rows, :] for m in range(count)] + [res, image]
+            accs = [acc + total(image * o) for acc, o in zip(accs, others)]
         packed = (
             jnp.where(lane8 == sub8, column(accs[:count]), 0.0)
             + jnp.where(lane8 == sub8 + 8, alongs, 0.0)
@@ -436,33 +438,30 @@
         step = whole(numerator / denominator)
         ys = [whole(y[:, m : m + 1]) for m in range(count)]
 
-        def update(x, _):
-            rows = pl.ds(pl.multiple_of(x * b, 8), b)
-            at = pl.ds(pl.multiple_of(base(x), 8), b)
+        for x in range(a):
+            rows = slice(x * b, x * b + b)
+            at = pl.ds(base(x), b)
             res = rwide[outer, at, :]
-            w = res - rem[at, :]
+            image = res - rem[at, :]
             for m in range(count):
-                w = w - ys[m] * img[m, rows, :]
-            res = res - step * w
+                image = image - ys[m] * img[m, rows, :]
+            res = res - step * image
             if outer + 1 < OUTER:
                 rwide[outer + 1, at, :] = res
             else:
                 res_ref[rows, :] = res
-            return 0
-
-        lax.fori_loop(0, a, update, 0)
-
-        def solution_update(x, _, step=step, ys=ys):
-            rows = pl.ds(pl.multiple_of(x * b, 8), b)
-            c = cbuf[pl.ds(pl.multiple_of(base(x), 8), b), :]
+
+        def solution_update(x, step=step, ys=ys):
+            rows = slice(x * b, x * b + b)
+            c = cbuf[pl.ds(base(x), b), :]
             for m in range(count):
                 c = c - ys[m] * rec_ref[m, rows, :].astype(F32)
             sol_ref[rows, :] = sol_ref[rows, :] + step * c
-            return 0
 
         later = solution_update
 
-    lax.fori_loop(0, a, later, 0)
+    for x in range(a):
+        later(x)
 
     for k in range(OUTER + 1):
         most = slots.at[k, pl.ds(0, n - 1)]

time: 45.1 us -> 42.2 us (0.936)
  Pallas kernels: 44.3 us -> 41.4 us
    pallas_call x1, Pallas kernels: 43.5 us -> 40.6 us  [local(): pl.pallas_call(functools.partial(kernel, gxn, gyn, count, a, b), out_shap...]
where the time goes in v1:
time: 42.2 us; the launch traced here: 42 us
  Pallas kernels  41.4 us (98%)
  between operations  0.64 us (2%)
    pallas_call x1, Pallas kernels, local(): pl.pallas_call(functools.partial(kernel, gxn, gyn, count, a, b), out_shap...  40.6 us

profile of v1, /device:TPU:0, one launch (start us, length us, event | category | flops | bytes accessed | tf_op | source)
XLA Modules:
  0.0 42.0 jit_solution(6337569140971056088)
XLA Ops:
  0.6 40.6 %shard_map.68 = (f32[512,128]{1,0:T(8,128)S(1)}, f32[512,128]{1,0:T(8,128)S(1)}) custom-call(f32[512,128]{1,0:T(8,128)} %bitcast.6, f32[512,128]{1,0:T(8,128)} %bitcast.7, bf16[8,512,128]{2,1,0:T(8,128)(2,1)} %bitcast.5, s32[16,32]{1,0:T(8,128)} %h_hbm.1, s32[16,32]{1,0:T(8,128)} %code_hbm.1), custom_call_target="tpu_custom_call" | custom-call | tf_op jit(solution)/shard_map/pallas_call | solution.py:499
  41.2 0.8 %shard_map.69 = (f32[512,128]{1,0:T(8,128)}, f32[512,128]{1,0:T(8,128)}) custom-call(f32[512,128]{1,0:T(8,128)S(1)} %get-tuple-element.6.sol_ref, f32[512,128]{1,0:T(8,128)S(1)} %get-tuple-element.7.res_ref), custom_call_target="tpu_custom_call" | custom-call | tf_op jit(solution)/shard_map/pallas_call | solution.py:551

commit v2 on v1

--- a/solution.py
+++ b/solution.py
@@ -10,6 +10,7 @@
 OUTER = 2
 SWEEPS = 3
 GHOST = SWEEPS
+NEAR = 2
 
 CENTER = 7.25
 HALF = 6.75
@@ -23,9 +24,9 @@
     rs_hbm, fg_hbm, rec_hbm, h_hbm, code_hbm,
     sol_ref, res_ref,
     rs_ref, fg_ref, rec_ref, ground, near_ground,
-    wide0, xsend0, ysend0, yrecv0, rwide, ysend, yrecv, csend, crecv,
+    wide0, xrecv0, ysend0, yrecv0, rwide, ysend, yrecv, csend, crecv,
     fwide, diag, uwide, dwide, rem, cbuf, img, psend, slots,
-    in_sem, gs_sem, gr_sem, hs_sem, hr_sem, ds_sem, dr_sem, ps_sem, pr_sem,
+    in_sem, gs_sem, gr_sem, hs_sem, hr_sem, ds_sem, dr_sem, ps_sem, pr_sem, known,
 ):
     lanes = 128
     S = b + 16
@@ -49,12 +50,33 @@
 
     barrier = pltpu.get_barrier_semaphore()
 
-    def greet(t, _):
-        peer = lax.rem(me + t, n)
-        pl.semaphore_signal(barrier, inc=1, **at_dev(peer // gyn, lax.rem(peer, gyn)))
-        return 0
-
-    lax.fori_loop(1, n, greet, 0)
+    gis = [lax.rem(gx + i, gxn) for i in range(gxn)]
+    gjs = [lax.rem(gy + j, gyn) for j in range(gyn)]
+
+    greeters = -1
+    for j in sorted(range(-NEAR, NEAR + 1), key=abs):
+        inside = jnp.logical_and(gy + j >= 0, gy + j < gyn)
+        greeters = greeters + jnp.where(inside, gxn, 0)
+
+        @pl.when(inside)
+        def _(j=j):
+            for i in range(gxn):
+                if i or j:
+                    pl.semaphore_signal(barrier, inc=1, **at_dev(gis[i], gy + j))
+
+    stages, reach = [], NEAR
+    while reach < gyn - 1:
+        stages.append(reach)
+        reach *= 2
+
+    def stage(k, act):
+        for side, j in enumerate((-stages[k], stages[k])):
+            @pl.when(jnp.logical_and(gy + j >= 0, gy + j < gyn))
+            def _(side=side, j=j):
+                if act == "signal":
+                    pl.semaphore_signal(known.at[k, 1 - side], inc=1, **at_dev(gx, gy + j))
+                else:
+                    pl.semaphore_wait(known.at[k, side], 1)
 
     def base0(x):
         return S * (x + 1) + 8
@@ -90,11 +112,11 @@
     def field_copy(m, s):
         w = wide0.at[m]
         src = (
-            xsend0.at[m, 0], xsend0.at[m, 1],
+            w.at[pl.ds(base0(0), b), :], w.at[pl.ds(base0(a - 1), b), :],
             ysend0.at[m, 0], ysend0.at[m, 1],
         )[s]
         dst = (
-            w.at[pl.ds(base0(a), b), :], w.at[pl.ds(base0(-1), b), :],
+            xrecv0.at[m, 1], xrecv0.at[m, 0],
             yrecv0.at[m, 1], yrecv0.at[m, 0],
         )[s]
         return pltpu.make_async_remote_copy(
@@ -142,7 +164,7 @@
             near_ground[s, 1] = jnp.zeros((a, b), jnp.int32)
             if s < 2:
                 for m in range(nf):
-                    wide0[m, pl.ds(base0(-1 if s == 0 else a), b), :] = zeros
+                    xrecv0[m, s] = zeros
                 for r in range(OUTER):
                     for i in range(GHOST):
                         rwide[r, pl.ds(base(i - GHOST if s == 0 else a + i), b), :] = zeros
@@ -182,51 +204,8 @@
     def fluid(x):
         return fwide[pl.ds(base(x), b), :]
 
-    def prepare(m):
-        loads[2 if m == count else 4 + m].wait()
-        w = wide0.at[m]
-        for x in range(a):
-            rows = slice(x * b, x * b + b)
-            v = fg_ref[rows, :] if m == count else rec_ref[m, rows, :].astype(F32)
-            w[pl.ds(base0(x), b), :] = v
-            if x == 0:
-                xsend0[m, 0] = v
-            if x == a - 1:
-                xsend0[m, 1] = v
-        ysend0[m, 0] = w[pl.ds(S + 8, a, stride=S), :]
-        ysend0[m, 1] = w[pl.ds(S + 8 + b - 1, a, stride=S), :]
-
-    order = [count] + list(range(count))
-    early = order[: (nf + 1) // 2]
-    for m in early:
-        prepare(m)
-    all_do(loads[:2], "wait")
-    pl.semaphore_wait(barrier, n - 1)
-    each((4, 5, 6, 7, 2, 3, 0, 1), lambda s: ground_copy(s).start())
-    for m in early:
-        each((2, 3, 0, 1), lambda s: field_copy(m, s).start())
-    for m in order[len(early) :]:
-        prepare(m)
-        each((2, 3, 0, 1), lambda s: field_copy(m, s).start())
-
-    for x in range(a):
-        mask_row(x, (ground,) * 3, x)
-
-    @pl.loop(0, nf)
-    def _(m):
-        for x in range(a):
-            at = pl.ds(base0(x), b)
-            wide0[m, at, :] = fluid(x) * wide0[m, at, :]
-
-    each(range(8), lambda s: ground_copy(opposite[s]).wait_recv())
-    for x in range(-GHOST, a + GHOST):
-        if x < 0:
-            trio, i = (near_ground.at[4], near_ground.at[0], near_ground.at[5]), a + x
-        elif x < a:
-            trio, i = (near_ground.at[2], ground, near_ground.at[3]), x
-        else:
-            trio, i = (near_ground.at[6], near_ground.at[1], near_ground.at[7]), x - a
-        mask_row(x, trio, i)
+    own_y = jnp.logical_and(lax.broadcasted_iota(jnp.int32, (S, lanes), 0) >= 8,
+                            lax.broadcasted_iota(jnp.int32, (S, lanes), 0) < b + 8)
 
     def near(w, at, size):
         c = w[pl.ds(at, size), :]
@@ -239,32 +218,64 @@
             + (up + down)
         )
 
-    for x in range(1 - GHOST, a + GHOST - 1):
+    all_do(loads[:2], "wait")
+    for x in (-1, a):
+        fwide[span(x), :] = jnp.zeros((S, lanes), F32)
+    for x in range(a):
+        mask_row(x, (ground,) * 3, x)
+        fwide[span(x), :] = jnp.where(own_y, fwide[span(x), :], 0.0)
+
+    def set_diag(x):
         f = fwide[span(x), :]
         diag[span(x), :] = f * (near(fwide, S * (x + GHOST), S) + diag[span(x), :]) + (1.0 - f)
 
-    def arrive(m):
-        each(range(4), lambda s: field_copy(m, opposite[s]).wait_recv())
+    def prepare(m):
+        loads[2 if m == count else 4 + m].wait()
+        w = wide0.at[m]
+        for x in range(a):
+            rows = slice(x * b, x * b + b)
+            v = fg_ref[rows, :] if m == count else rec_ref[m, rows, :].astype(F32)
+            w[pl.ds(base0(x), b), :] = fluid(x) * v
+        ysend0[m, 0] = w[pl.ds(S + 8, a, stride=S), :]
+        ysend0[m, 1] = w[pl.ds(S + 8 + b - 1, a, stride=S), :]
+
+    order = [count] + list(range(count))
+    early = order[: (nf + 1) // 2]
+    for m in early:
+        prepare(m)
+    pl.semaphore_wait(barrier, greeters)
+    each((4, 5, 6, 7, 2, 3, 0, 1), lambda s: ground_copy(s).start())
+    for m in early:
+        each((2, 3, 0, 1), lambda s: field_copy(m, s).start())
+    for k in range(len(stages)):
+        if k == 0:
+            stage(k, "signal")
+    for m in order[len(early) :]:
+        prepare(m)
+        each((2, 3, 0, 1), lambda s: field_copy(m, s).start())
+
+    zeros_a = jnp.zeros((a, lanes), F32)
+    for m in range(nf):
         w = wide0.at[m]
         for x in (-1, a):
-            at = pl.ds(base0(x), b)
-            w[at, :] = fluid(x) * w[at, :]
-        for i, x in enumerate((-1, b)):
-            w[pl.ds(base0(0) + x, a, stride=S), :] = (
-                fwide[pl.ds(base(0) + x, a, stride=S), :] * yrecv0[m, i]
-            )
+            w[pl.ds(base0(x), b), :] = zeros
+        for y in (-1, b):
+            w[pl.ds(base0(0) + y, a, stride=S), :] = zeros_a
+    for x in range(a):
+        set_diag(x)
+
+    zero8 = jnp.zeros((8, lanes), F32)
+
+    def tiles(v):
+        return [v[i : i + 8] for i in range(0, v.shape[0], 8)]
 
     def total(v):
-        out = v[0:8]
-        for i in range(8, b, 8):
-            out = out + v[i : i + 8]
-        return out
-
-    zero8 = jnp.zeros((8, lanes), F32)
+        return functools.reduce(jnp.add, tiles(v))
+
     table = {}
     loads[3].wait()
-    for m in order:
-        arrive(m)
+    waited = 0
+    for turn, m in enumerate(order):
         sums = [zero8] * (m + 2)
         for x in range(a):
             rows = slice(x * b, x * b + b)
@@ -275,12 +286,40 @@
                 continue
             v = dg * rec_ref[m, rows, :].astype(F32) - flow
             img[m, rows, :] = v
-            others = [img[q, rows, :] for q in range(m)] + [v, res_ref[rows, :]]
-            sums = [acc + total(v * o) for acc, o in zip(sums, others)]
+            if 0 < x < a - 1:
+                inner = tiles(v)
+                inner[0] = jnp.where(sub8 > 0, inner[0], 0.0)
+                inner[-1] = jnp.where(sub8 < 7, inner[-1], 0.0)
+                others = [img[q, rows, :] for q in range(m)] + [v, res_ref[rows, :]]
+                sums = [
+                    acc + functools.reduce(jnp.add, [i * j for i, j in zip(inner, tiles(o))])
+                    for acc, o in zip(sums, others)
+                ]
         if m < count:
-            for q in range(m + 1):
-                table[(q, m)] = sums[q]
-            table[m] = sums[m + 1]
+            table[m] = sums
+        if turn in (2, 6) and waited < len(stages):
+            stage(waited, "wait")
+            waited += 1
+            if waited < len(stages):
+                stage(waited, "signal")
+    while waited < len(stages):
+        stage(waited, "wait")
+        waited += 1
+        if waited < len(stages):
+            stage(waited, "signal")
+
+    each(range(8), lambda s: ground_copy(opposite[s]).wait_recv())
+    for x in range(-GHOST, a + GHOST):
+        if x < 0:
+            trio, i = (near_ground.at[4], near_ground.at[0], near_ground.at[5]), a + x
+        elif x < a:
+            trio, i = (near_ground.at[2], ground, near_ground.at[3]), x
+        else:
+            trio, i = (near_ground.at[6], near_ground.at[1], near_ground.at[7]), x - a
+        mask_row(x, trio, i)
+
+    for x in range(1 - GHOST, a + GHOST - 1):
+        set_diag(x)
 
     def column(items):
         rows = [jnp.sum(v, axis=0, keepdims=True) for v in items]
@@ -288,17 +327,38 @@
             rows.append(jnp.zeros((8 - len(rows), lanes), F32))
         return jnp.sum(jnp.concatenate(rows, axis=0), axis=1, keepdims=True)
 
+    sub_a = lax.broadcasted_iota(jnp.int32, (a, lanes), 0)
+    mid_a = jnp.logical_and(sub_a > 0, sub_a < a - 1)
+    ends = [slice(x * b, x * b + b) for x in (0, a - 1)]
+    strips = [pl.ds(y, a, stride=b) for y in (0, b - 1)]
     packed = zero8
-    for q in range(count + 1):
-        items = (
-            [table[(min(m, q), max(m, q))] for m in range(count)]
-            if q < count
-            else [table[m] for m in range(count)]
-        )
-        packed = packed + jnp.where(lane8 == 16 * sub8 + q, column(items), 0.0)
-
-    gis = [lax.rem(gx + i, gxn) for i in range(gxn)]
-    gjs = [lax.rem(gy + j, gyn) for j in range(gyn)]
+    starts = []
+    for m in order:
+        each(range(4), lambda s: field_copy(m, opposite[s]).wait_recv())
+        out = res_ref if m == count else img.at[m]
+        sign = -1.0 if m == count else 1.0
+        for i, (x, g) in enumerate(((0, -1), (a - 1, a))):
+            add = fluid(g) * wide0[m, pl.ds(base0(x), b), :] - fluid(x) * xrecv0[m, i]
+            out[ends[i], :] = out[ends[i], :] + sign * add
+        for i, (y, g) in enumerate(((0, -1), (b - 1, b))):
+            f_out = fwide[pl.ds(base(0) + g, a, stride=S), :]
+            f_own = fwide[pl.ds(base(0) + y, a, stride=S), :]
+            add = f_out * ysend0[m, i] - f_own * yrecv0[m, i]
+            out[strips[i], :] = out[strips[i], :] + sign * add
+        if m == count:
+            continue
+        sums = table[m]
+        for part in ends + strips:
+            v = img[m, part, :]
+            others = [img[q, part, :] for q in range(m)] + [v, res_ref[part, :]]
+            if part in strips:
+                v = jnp.where(mid_a, v, 0.0)
+            sums = [acc + total(v * o) for acc, o in zip(sums, others)]
+        pair = jnp.logical_or(lane8 == 16 * sub8 + m, lane8 == 16 * m + sub8)
+        packed = packed + jnp.where(jnp.logical_and(pair, sub8 <= m), column(sums[: m + 1]), 0.0)
+        starts.append(sums[m + 1])
+    packed = packed + jnp.where(lane8 == 16 * sub8 + count, column(starts), 0.0)
+
     far_first = sorted(
         [(i, j) for i in range(gxn) for j in range(gyn) if i or j],
         key=lambda t: (abs(t[1] - gyn // 2), abs(t[0] - gxn // 2)),
@@ -534,6 +594,7 @@
                 dma((OUTER, 8, GHOST)),
                 dma((OUTER + 1,)),
                 dma((OUTER + 1,)),
+                pltpu.SemaphoreType.REGULAR((max(gyn.bit_length(), 1), 2)),
             ],
             compiler_params=pltpu.CompilerParams(
                 collective_id=0, has_side_effects=True, vmem_limit_bytes=32 * 2**20

time: 42.2 us -> 40.3 us (0.955)
  Pallas kernels: 41.4 us -> 39.4 us
    pallas_call x1, Pallas kernels: 40.6 us -> 38.6 us  [local(): pl.pallas_call(functools.partial(kernel, gxn, gyn, count, a, b), out_shap...]
where the time goes in v2:
time: 40.3 us; the launch traced here: 40 us
  Pallas kernels  39.4 us (98%)
  between operations  0.64 us (2%)
    pallas_call x1, Pallas kernels, local(): pl.pallas_call(functools.partial(kernel, gxn, gyn, count, a, b), out_shap...  38.6 us
    pallas_call x1, Pallas kernels, local(): pl.pallas_call(store, out_shape=(field, field), in_specs=[vm] * 2, out_sp...  0.81 us

profile of v2, /device:TPU:0, one launch (start us, length us, event | category | flops | bytes accessed | tf_op | source)
XLA Modules:
  0.0 40.0 jit_solution(3385611189869659979)
XLA Ops:
  0.6 38.6 %shard_map.68 = (f32[512,128]{1,0:T(8,128)S(1)}, f32[512,128]{1,0:T(8,128)S(1)}) custom-call(f32[512,128]{1,0:T(8,128)} %bitcast.6, f32[512,128]{1,0:T(8,128)} %bitcast.7, bf16[8,512,128]{2,1,0:T(8,128)(2,1)} %bitcast.5, s32[16,32]{1,0:T(8,128)} %h_hbm.1, s32[16,32]{1,0:T(8,128)} %code_hbm.1), custom_call_target="tpu_custom_call" | custom-call | tf_op jit(solution)/shard_map/pallas_call | solution.py:559
  39.2 0.8 %shard_map.69 = (f32[512,128]{1,0:T(8,128)}, f32[512,128]{1,0:T(8,128)}) custom-call(f32[512,128]{1,0:T(8,128)S(1)} %get-tuple-element.6.sol_ref, f32[512,128]{1,0:T(8,128)S(1)} %get-tuple-element.7.res_ref), custom_call_target="tpu_custom_call" | custom-call | tf_op jit(solution)/shard_map/pallas_call | solution.py:612

commit v3 on v2

--- a/solution.py
+++ b/solution.py
@@ -26,7 +26,8 @@
     rs_ref, fg_ref, rec_ref, ground, near_ground,
     wide0, xrecv0, ysend0, yrecv0, rwide, ysend, yrecv, csend, crecv,
     fwide, diag, uwide, dwide, rem, cbuf, img, psend, slots,
-    in_sem, gs_sem, gr_sem, hs_sem, hr_sem, ds_sem, dr_sem, ps_sem, pr_sem, known,
+    wown, wysend, wcsend, wxrecv, wyrecv, wcrecv, iysend, icsend, ixrecv, iyrecv, icrecv,
+    in_sem, gs_sem, gr_sem, hs_sem, hr_sem, ds_sem, dr_sem, ps_sem, pr_sem, ws_sem, wr_sem, is_sem, ir_sem, known,
 ):
     lanes = 128
     S = b + 16
@@ -124,8 +125,13 @@
             send_sem=hs_sem.at[m, s], recv_sem=hr_sem.at[m, opposite[s]], **peers[s],
         )
 
-    def deep_copies(r, s):
-        w = rwide.at[r]
+    def send_to(s, src, dst, sends, recvs):
+        return pltpu.make_async_remote_copy(
+            src_ref=src, dst_ref=dst, send_sem=sends, recv_sem=recvs, **peers[s]
+        )
+
+    def deep_copies(s):
+        w = rwide.at[0]
         if s < 2:
             pieces = [
                 (
@@ -135,16 +141,34 @@
                 for i in range(GHOST)
             ]
         elif s < 4:
-            pieces = [(ysend.at[r, s - 2], yrecv.at[r, 3 - s])]
+            pieces = [(ysend.at[s - 2], yrecv.at[3 - s])]
         else:
-            pieces = [(csend.at[r, s - 4], crecv.at[r, opposite[s] - 4])]
+            pieces = [(csend.at[s - 4], crecv.at[opposite[s] - 4])]
         return [
-            pltpu.make_async_remote_copy(
-                src_ref=p, dst_ref=q,
-                send_sem=ds_sem.at[r, s, i], recv_sem=dr_sem.at[r, opposite[s], i], **peers[s],
-            )
+            send_to(s, p, q, ds_sem.at[s, i], dr_sem.at[opposite[s], i])
             for i, (p, q) in enumerate(pieces)
         ]
+
+    def face(field, s):
+        return field.at[pl.ds(0 if s == 0 else (a - GHOST) * b, GHOST * b), :]
+
+    def w_copy(s):
+        if s < 2:
+            src, dst = face(wown.at[0], s), wxrecv.at[1 - s]
+        elif s < 4:
+            src, dst = wysend.at[s - 2], wyrecv.at[3 - s]
+        else:
+            src, dst = wcsend.at[s - 4], wcrecv.at[opposite[s] - 4]
+        return send_to(s, src, dst, ws_sem.at[s], wr_sem.at[opposite[s]])
+
+    def image_copy(m, s):
+        if s < 2:
+            src, dst = face(img.at[m], s), ixrecv.at[m, 1 - s]
+        elif s < 4:
+            src, dst = iysend.at[m, s - 2], iyrecv.at[m, 3 - s]
+        else:
+            src, dst = icsend.at[s - 4], icrecv.at[opposite[s] - 4]
+        return send_to(s, src, dst, is_sem.at[m, s], ir_sem.at[m, opposite[s]])
 
     def each(sides, act):
         for s in sides:
@@ -157,28 +181,6 @@
             getattr(cp, what)()
 
     zeros = jnp.zeros((b, lanes), F32)
-    for s in range(8):
-        @pl.when(jnp.logical_not(have[s]))
-        def _(s=s):
-            near_ground[s, 0] = jnp.full((a, b), 255, jnp.int32)
-            near_ground[s, 1] = jnp.zeros((a, b), jnp.int32)
-            if s < 2:
-                for m in range(nf):
-                    xrecv0[m, s] = zeros
-                for r in range(OUTER):
-                    for i in range(GHOST):
-                        rwide[r, pl.ds(base(i - GHOST if s == 0 else a + i), b), :] = zeros
-            elif s < 4:
-                for m in range(nf):
-                    yrecv0[m, s - 2] = jnp.zeros((a, lanes), F32)
-                for r in range(OUTER):
-                    for i in range(GHOST):
-                        yrecv[r, s - 2, i] = jnp.zeros((a, lanes), F32)
-            else:
-                for r in range(OUTER):
-                    for i in range(3):
-                        crecv[r, s - 4, i] = jnp.zeros((1, lanes), F32)
-
     ones = jnp.ones((b, lanes), jnp.bfloat16)
     yi = lax.broadcasted_iota(jnp.int32, (S, b), 0)
     ji = lax.broadcasted_iota(jnp.int32, (S, b), 1)
@@ -255,6 +257,32 @@
         each((2, 3, 0, 1), lambda s: field_copy(m, s).start())
 
     zeros_a = jnp.zeros((a, lanes), F32)
+    for s in range(8):
+        @pl.when(jnp.logical_not(have[s]))
+        def _(s=s):
+            near_ground[s, 0] = jnp.full((a, b), 255, jnp.int32)
+            near_ground[s, 1] = jnp.zeros((a, b), jnp.int32)
+            if s < 2:
+                wxrecv[s] = jnp.zeros((GHOST * b, lanes), F32)
+                for m in range(nf):
+                    xrecv0[m, s] = zeros
+                for m in range(count):
+                    ixrecv[m, s] = jnp.zeros((GHOST * b, lanes), F32)
+                for i in range(GHOST):
+                    rwide[0, pl.ds(base(i - GHOST if s == 0 else a + i), b), :] = zeros
+            elif s < 4:
+                wyrecv[s - 2] = jnp.zeros((GHOST * a, lanes), F32)
+                for m in range(nf):
+                    yrecv0[m, s - 2] = zeros_a
+                for m in range(count):
+                    iyrecv[m, s - 2] = jnp.zeros((GHOST * a, lanes), F32)
+                for i in range(GHOST):
+                    yrecv[s - 2, i] = zeros_a
+            else:
+                crecv[s - 4] = jnp.zeros((8, lanes), F32)
+                wcrecv[s - 4] = jnp.zeros((8, lanes), F32)
+                icrecv[s - 4] = jnp.zeros((count * GHOST, lanes), F32)
+
     for m in range(nf):
         w = wide0.at[m]
         for x in (-1, a):
@@ -327,6 +355,26 @@
             rows.append(jnp.zeros((8 - len(rows), lanes), F32))
         return jnp.sum(jnp.concatenate(rows, axis=0), axis=1, keepdims=True)
 
+    bits = ((0, 0), (0, 1), (1, 0))
+
+    def corner_at(s, p, q):
+        return p if steps[s][0] < 0 else a - 1 - p, q if steps[s][1] < 0 else b - 1 - q
+
+    def take_strips(field, out):
+        for i in range(GHOST):
+            for side, y in enumerate((i, b - 1 - i)):
+                out[side, i * a : (i + 1) * a, :] = field[pl.ds(y, a, stride=b), :]
+
+    def image_strips(fields):
+        for m in fields:
+            take_strips(img.at[m], iysend.at[m])
+
+    def share(fields):
+        for m in fields:
+            each((2, 3, 0, 1), lambda s: image_copy(m, s).start())
+
+    first, second = count // 4, count * 3 // 4
+
     sub_a = lax.broadcasted_iota(jnp.int32, (a, lanes), 0)
     mid_a = jnp.logical_and(sub_a > 0, sub_a < a - 1)
     ends = [slice(x * b, x * b + b) for x in (0, a - 1)]
@@ -357,6 +405,9 @@
         pair = jnp.logical_or(lane8 == 16 * sub8 + m, lane8 == 16 * m + sub8)
         packed = packed + jnp.where(jnp.logical_and(pair, sub8 <= m), column(sums[: m + 1]), 0.0)
         starts.append(sums[m + 1])
+        if m < first:
+            image_strips([m])
+            share([m])
     packed = packed + jnp.where(lane8 == 16 * sub8 + count, column(starts), 0.0)
 
     far_first = sorted(
@@ -364,7 +415,7 @@
         key=lambda t: (abs(t[1] - gyn // 2), abs(t[0] - gxn // 2)),
     )
 
-    def all_sum(k, row):
+    def sum_start(k, row):
         psend[k] = row
         slots[k, me] = row
 
@@ -384,76 +435,106 @@
                 return 0
 
             lax.fori_loop(1, n, step, 0)
+    def sum_done(k):
         most = slots.at[k, pl.ds(0, n - 1)]
         pltpu.make_async_copy(most, most, pr_sem.at[k]).wait()
-        out = jnp.sum(slots[k], axis=0)
-        return out
-
-    row = all_sum(0, jnp.sum(packed, axis=0, keepdims=True))
+        return jnp.sum(slots[k], axis=0)
+
+    def widened(v, size):
+        return jnp.broadcast_to(v, (size, lanes))
+
+    sum_start(0, jnp.sum(packed, axis=0, keepdims=True))
+    image_strips(range(first, second))
+    share(range(first, second))
+    for s in range(4, 8):
+        for i, (p, q) in enumerate(bits):
+            x, y = corner_at(s, p, q)
+            for m in range(count):
+                icsend[s - 4, pl.ds(GHOST * m + i, 1), :] = img[m, pl.ds(x * b + y, 1), :]
+    each(range(4, 8), lambda s: image_copy(0, s).start())
+    image_strips(range(second, count))
+    for s in range(4):
+        csend[s] = zero8
+        wcsend[s] = zero8
+    row = sum_done(0)
 
     wrow = jnp.broadcast_to(row, (8, lanes))
-    mat = zero8
+    gram = zero8
     for m in range(count):
         moved = wrow if m == 0 else pltpu.roll(wrow, lanes - 16 * m, 1)
-        mat = jnp.where(sub8 == m, moved, mat)
-    mat = jnp.where(lane8 <= count, mat, 0.0) + jnp.where(lane8 == 16 + sub8, 1.0, 0.0)
+        gram = jnp.where(sub8 == m, moved, gram)
+    cols = [jnp.broadcast_to(gram[:, k : k + 1], (8, lanes)) for k in range(count + 1)]
+    start = cols[count]
+    cols += [jnp.where(sub8 == k, 1.0, 0.0) for k in range(count)]
     for k in range(count):
-        pivot = mat[k : k + 1, :] / mat[k : k + 1, k : k + 1]
-        mat = jnp.where(sub8 == k, pivot, mat - mat[:, k : k + 1] * pivot)
-    inverse = pltpu.roll(mat, lanes - 16, 1)
-
-    def whole(v):
-        return jnp.concatenate([jnp.broadcast_to(v, (8, lanes))] * (b // 8), axis=0)
-
-    coeffs = [whole(mat[m : m + 1, count : count + 1]) for m in range(count)]
+        this = cols[k]
+        scale = 1.0 / widened(this[k : k + 1], 8)
+        for j in list(range(k + 1, count + 1)) + list(range(count + 1, count + 2 + k)):
+            pivot = widened(cols[j][k : k + 1], 8) * scale
+            cols[j] = jnp.where(sub8 == k, pivot, cols[j] - this * pivot)
+    coef = cols[count]
+    coeffs = [coef[m : m + 1] for m in range(count)]
 
     for x in range(a):
         rows = slice(x * b, x * b + b)
         res = res_ref[rows, :]
         for m in range(count):
-            res = res - coeffs[m] * img[m, rows, :]
+            res = res - widened(coeffs[m], b) * img[m, rows, :]
         rwide[0, pl.ds(base(x), b), :] = res
 
-    def first_solution(x):
+    w = rwide.at[0]
+    for i in range(GHOST):
+        ysend[0, i] = w[pl.ds(base(0) + i, a, stride=S), :]
+        ysend[1, i] = w[pl.ds(base(0) + b - 1 - i, a, stride=S), :]
+    for s in range(4, 8):
+        for i, (p, q) in enumerate(bits):
+            x, y = corner_at(s, p, q)
+            csend[s - 4, pl.ds(i, 1), :] = w[pl.ds(base(x) + y, 1), :]
+    each((4, 5, 6, 7, 2, 3, 0, 1), lambda s: all_do(deep_copies(s), "start"))
+
+    inverse = zero8
+    for k in range(count):
+        inverse = jnp.where(lane8 == k, cols[count + 1 + k], inverse)
+    gram = jnp.where(lane8 < count, gram, 0.0)
+
+    def times(matrix, row):
+        return jnp.sum(matrix * row, axis=1, keepdims=True)
+
+    def as_row(col):
+        return jnp.sum(jnp.where(lane8 == sub8, col, 0.0), axis=0, keepdims=True)
+
+    along = start - times(gram, as_row(coef))
+
+    for x in range(a):
         rows = slice(x * b, x * b + b)
         sol = fg_ref[rows, :]
         for m in range(count):
-            sol = sol + coeffs[m] * rec_ref[m, rows, :].astype(F32)
+            sol = sol + widened(coeffs[m], b) * rec_ref[m, rows, :].astype(F32)
         sol_ref[rows, :] = sol
 
-    later = first_solution
-
-    bits = ((0, 0), (0, 1), (1, 0))
+    each((2, 3), lambda s: all_do(deep_copies(s), "wait_send"))
+    share(range(second, count))
+    each(range(8), lambda s: all_do(deep_copies(opposite[s]), "wait_recv"))
+
+    def put_strip(w, side, i, v):
+        y = -1 - i if side == 0 else b + i
+        w[pl.ds(base(0) + y, a, stride=S), :] = v
+
+    def put_corner(w, s, v):
+        for i, (p, q) in enumerate(bits):
+            x = -1 - p if steps[s][0] < 0 else a + p
+            y = -1 - q if steps[s][1] < 0 else b + q
+            w[pl.ds(base(x) + y, 1), :] = v[i : i + 1]
+
+    for i in range(GHOST):
+        for side in range(2):
+            put_strip(w, side, i, yrecv[side, i])
+    for s in range(4, 8):
+        put_corner(w, s, crecv[s - 4])
 
     for outer in range(OUTER):
+        last = outer + 1 == OUTER
         w = rwide.at[outer]
-        for i in range(GHOST):
-            ysend[outer, 0, i] = w[pl.ds(base(0) + i, a, stride=S), :]
-            ysend[outer, 1, i] = w[pl.ds(base(0) + b - 1 - i, a, stride=S), :]
-        for s in range(4, 8):
-            for i, (p, q) in enumerate(bits):
-                x = p if steps[s][0] < 0 else a - 1 - p
-                y = q if steps[s][1] < 0 else b - 1 - q
-                csend[outer, s - 4, i] = w[pl.ds(base(x) + y, 1), :]
-        each((4, 5, 6, 7, 2, 3, 0, 1), lambda s: all_do(deep_copies(outer, s), "start"))
-        for x in range(a):
-            later(x)
-
-        accs = [zero8] * count
-        for x in range(a):
-            rows = slice(x * b, x * b + b)
-            res = w[pl.ds(base(x), b), :]
-            accs = [acc + total(img[m, rows, :] * res) for m, acc in enumerate(accs)]
-        alongs = column(accs)
-        each(range(8), lambda s: all_do(deep_copies(outer, opposite[s]), "wait_recv"))
-        for i in range(GHOST):
-            w[pl.ds(base(0) - 1 - i, a, stride=S), :] = yrecv[outer, 0, i]
-            w[pl.ds(base(0) + b + i, a, stride=S), :] = yrecv[outer, 1, i]
-        for s in range(4, 8):
-            for i, (p, q) in enumerate(bits):
-                x = -1 - p if steps[s][0] < 0 else a + p
-                y = -1 - q if steps[s][1] < 0 else b + q
-                w[pl.ds(base(x) + y, 1), :] = crecv[outer, s - 4, i]
         for x in range(-GHOST, a + GHOST):
             uwide[0, span(x), :] = fwide[span(x), :] * (w[span(x), :] * (1.0 / CENTER))
         rho = 1.0 / SIGMA
@@ -467,7 +548,10 @@
                 old = w[rows, :] if sweep == 0 else rem[rows, :]
                 d = old * (1.0 / CENTER) if sweep == 0 else dwide[rows, :]
                 left = old - (diag[rows, :] * d - f * near(uwide.at[sweep], at, size))
-                cbuf[rows, :] = d if sweep == 0 else cbuf[rows, :] + d
+                if 0 <= x < a:
+                    own = slice(x * b, x * b + b)
+                    mine = d if grow == 0 else d[8 : 8 + b]
+                    cbuf[outer, own, :] = mine if sweep == 0 else cbuf[outer, own, :] + mine
                 rem[rows, :] = left
                 if sweep + 1 < SWEEPS:
                     d = (rho_new * rho) * d + (2.0 * rho_new / HALF) * left
@@ -479,49 +563,88 @@
         for x in range(a):
             rows = slice(x * b, x * b + b)
             at = pl.ds(base(x), b)
-            res = rwide[outer, at, :]
+            res = w[at, :]
             image = res - rem[at, :]
+            wown[outer, rows, :] = image
             others = [img[m, rows, :] for m in range(count)] + [res, image]
             accs = [acc + total(image * o) for acc, o in zip(accs, others)]
         packed = (
             jnp.where(lane8 == sub8, column(accs[:count]), 0.0)
-            + jnp.where(lane8 == sub8 + 8, alongs, 0.0)
             + jnp.where(lane8 == sub8 + 16, column(accs[count:]), 0.0)
         )
-        row = all_sum(1 + outer, jnp.sum(packed, axis=0, keepdims=True))
-        onto = jnp.sum(jnp.where(lane8 == sub8, jnp.broadcast_to(row, (8, lanes)), 0.0), axis=1, keepdims=True)
-        y = jnp.sum(onto * inverse, axis=0, keepdims=True)
-        y = jnp.where(row1 < count, y, 0.0)
-        along = pltpu.roll(jnp.broadcast_to(row, (8, lanes)), lanes - 8, 1)[0:1]
-        numerator = row[:, 16:17] - jnp.sum(y * along, axis=1, keepdims=True)
-        denominator = row[:, 17:18] - jnp.sum(y * row, axis=1, keepdims=True)
-        step = whole(numerator / denominator)
-        ys = [whole(y[:, m : m + 1]) for m in range(count)]
+        sum_start(1 + outer, jnp.sum(packed, axis=0, keepdims=True))
+        if not last:
+            take_strips(wown.at[outer], wysend)
+            for s in range(4, 8):
+                for i, (p, q) in enumerate(bits):
+                    x, y = corner_at(s, p, q)
+                    wcsend[s - 4, pl.ds(i, 1), :] = wown[outer, pl.ds(x * b + y, 1), :]
+            each((4, 5, 6, 7, 2, 3, 0, 1), lambda s: w_copy(s).start())
+        else:
+            for x in range(a):
+                earlier(x)
+        row = sum_done(1 + outer)
+
+        onto_row = jnp.where(lane8 < count, jnp.broadcast_to(row, (8, lanes)), 0.0)
+        y = times(inverse, onto_row)
+        onto = jnp.sum(jnp.where(lane8 == sub8, onto_row, 0.0), axis=1, keepdims=True)
+        numerator = row[:, 16:17] - jnp.sum(y * along, axis=0, keepdims=True)[:, 0:1]
+        denominator = row[:, 17:18] - jnp.sum(y * onto, axis=0, keepdims=True)
+        step = jnp.broadcast_to(numerator / denominator, (1, lanes))
+        y = jnp.broadcast_to(y, (8, lanes))
+        ys = [y[m : m + 1] for m in range(count)]
+
+        def stepped(res, image, parts):
+            size = res.shape[0]
+            for m in range(count):
+                image = image - widened(ys[m], size) * parts(m)
+            return res - widened(step, size) * image
 
         for x in range(a):
             rows = slice(x * b, x * b + b)
             at = pl.ds(base(x), b)
-            res = rwide[outer, at, :]
-            image = res - rem[at, :]
+            res = stepped(w[at, :], wown[outer, rows, :], lambda m: img[m, rows, :])
+            if last:
+                res_ref[rows, :] = res
+            else:
+                rwide[outer + 1, at, :] = res
+
+        def solution_update(x, outer=outer, step=step, ys=ys):
+            rows = slice(x * b, x * b + b)
+            c = cbuf[outer, rows, :]
             for m in range(count):
-                image = image - ys[m] * img[m, rows, :]
-            res = res - step * image
-            if outer + 1 < OUTER:
-                rwide[outer + 1, at, :] = res
-            else:
-                res_ref[rows, :] = res
-
-        def solution_update(x, step=step, ys=ys):
-            rows = slice(x * b, x * b + b)
-            c = cbuf[pl.ds(base(x), b), :]
-            for m in range(count):
-                c = c - ys[m] * rec_ref[m, rows, :].astype(F32)
-            sol_ref[rows, :] = sol_ref[rows, :] + step * c
-
-        later = solution_update
-
-    for x in range(a):
-        later(x)
+                c = c - widened(ys[m], b) * rec_ref[m, rows, :].astype(F32)
+            sol_ref[rows, :] = sol_ref[rows, :] + widened(step, b) * c
+
+        if last:
+            for x in range(a):
+                solution_update(x)
+            continue
+        earlier = solution_update
+
+        for m in range(count):
+            each(range(4), lambda s: image_copy(m, opposite[s]).wait_recv())
+        each(range(4, 8), lambda s: image_copy(0, opposite[s]).wait_recv())
+        each(range(8), lambda s: w_copy(opposite[s]).wait_recv())
+        new = rwide.at[outer + 1]
+        for side in range(2):
+            for i in range(GHOST):
+                at = pl.ds(base(i - GHOST if side == 0 else a + i), b)
+                rows = slice(i * b, i * b + b)
+                new[at, :] = stepped(
+                    w[at, :], wxrecv[side, rows, :], lambda m: ixrecv[m, side, rows, :]
+                )
+                rows = slice(i * a, i * a + a)
+                put_strip(new, side, i, stepped(
+                    yrecv[side, i], wyrecv[side, rows, :], lambda m: iyrecv[m, side, rows, :]
+                ))
+        for s in range(4, 8):
+            c = s - 4
+            put_corner(new, s, stepped(
+                crecv[c, :GHOST], wcrecv[c, :GHOST],
+                lambda m: icrecv[c, GHOST * m : GHOST * m + GHOST, :],
+            ))
+        along = along - step * (onto - times(gram, as_row(y)))
 
     for k in range(OUTER + 1):
         most = slots.at[k, pl.ds(0, n - 1)]
@@ -529,8 +652,11 @@
     each(range(8), lambda s: ground_copy(s).wait_send())
     for m in range(nf):
         each(range(4), lambda s: field_copy(m, s).wait_send())
-    for r in range(OUTER):
-        each(range(8), lambda s: all_do(deep_copies(r, s), "wait_send"))
+    each((0, 1, 4, 5, 6, 7), lambda s: all_do(deep_copies(s), "wait_send"))
+    each(range(8), lambda s: w_copy(s).wait_send())
+    for m in range(count):
+        each(range(4), lambda s: image_copy(m, s).wait_send())
+    each(range(4, 8), lambda s: image_copy(0, s).wait_send())
 
 
 def store(sol_ref, res_ref, sol_out, res_out, sem):
@@ -572,28 +698,43 @@
                 pltpu.VMEM((count + 1, 2, a, nz), F32),
                 pltpu.VMEM((count + 1, 2, a, nz), F32),
                 pltpu.VMEM((OUTER,) + wide_f.shape, F32),
-                pltpu.VMEM((OUTER, 2, GHOST, a, nz), F32),
-                pltpu.VMEM((OUTER, 2, GHOST, a, nz), F32),
-                pltpu.VMEM((OUTER, 4, 3, 1, nz), F32),
-                pltpu.VMEM((OUTER, 4, 3, 1, nz), F32),
+                pltpu.VMEM((2, GHOST, a, nz), F32),
+                pltpu.VMEM((2, GHOST, a, nz), F32),
+                pltpu.VMEM((4, 8, nz), F32),
+                pltpu.VMEM((4, 8, nz), F32),
                 wide_f,
                 wide_f,
                 pltpu.VMEM((SWEEPS,) + wide_f.shape, F32),
                 wide_f,
                 wide_f,
-                wide_f,
+                pltpu.VMEM((OUTER, a * b, nz), F32),
                 pltpu.VMEM((count, a * b, nz), F32),
                 pltpu.VMEM((OUTER + 1, 1, nz), F32),
                 pltpu.VMEM((OUTER + 1, n, 1, nz), F32),
+                pltpu.VMEM((OUTER, a * b, nz), F32),
+                pltpu.VMEM((2, GHOST * a, nz), F32),
+                pltpu.VMEM((4, 8, nz), F32),
+                pltpu.VMEM((2, GHOST * b, nz), F32),
+                pltpu.VMEM((2, GHOST * a, nz), F32),
+                pltpu.VMEM((4, 8, nz), F32),
+                pltpu.VMEM((count, 2, GHOST * a, nz), F32),
+                pltpu.VMEM((4, count * GHOST, nz), F32),
+                pltpu.VMEM((count, 2, GHOST * b, nz), F32),
+                pltpu.VMEM((count, 2, GHOST * a, nz), F32),
+                pltpu.VMEM((4, count * GHOST, nz), F32),
                 dma((4 + count,)),
                 dma((8,)),
                 dma((8,)),
                 dma((count + 1, 4)),
                 dma((count + 1, 4)),
-                dma((OUTER, 8, GHOST)),
-                dma((OUTER, 8, GHOST)),
+                dma((8, GHOST)),
+                dma((8, GHOST)),
                 dma((OUTER + 1,)),
                 dma((OUTER + 1,)),
+                dma((8,)),
+                dma((8,)),
+                dma((count, 8)),
+                dma((count, 8)),
                 pltpu.SemaphoreType.REGULAR((max(gyn.bit_length(), 1), 2)),
             ],
             compiler_params=pltpu.CompilerParams(

time: 40.3 us -> 38.6 us (0.958)
  Pallas kernels: 39.4 us -> 37.7 us
    pallas_call x1, Pallas kernels: 38.6 us -> 36.9 us  [local(): pl.pallas_call(functools.partial(kernel, gxn, gyn, count, a, b), out_shap...]
where the time goes in v3:
time: 38.6 us; the launch traced here: 38.3 us
  Pallas kernels  37.7 us (98%)
  between operations  0.64 us (2%)
    pallas_call x1, Pallas kernels, local(): pl.pallas_call(functools.partial(kernel, gxn, gyn, count, a, b), out_shap...  36.9 us
    pallas_call x1, Pallas kernels, local(): pl.pallas_call(store, out_shape=(field, field), in_specs=[vm] * 2, out_sp...  0.81 us

profile of v3, /device:TPU:0, one launch (start us, length us, event | category | flops | bytes accessed | tf_op | source)
XLA Modules:
  0.0 38.3 jit_solution(9226360629322146425)
XLA Ops:
  0.6 36.9 %shard_map.68 = (f32[512,128]{1,0:T(8,128)S(1)}, f32[512,128]{1,0:T(8,128)S(1)}) custom-call(f32[512,128]{1,0:T(8,128)} %bitcast.6, f32[512,128]{1,0:T(8,128)} %bitcast.7, bf16[8,512,128]{2,1,0:T(8,128)(2,1)} %bitcast.5, s32[16,32]{1,0:T(8,128)} %h_hbm.1, s32[16,32]{1,0:T(8,128)} %code_hbm.1), custom_call_target="tpu_custom_call" | custom-call | tf_op jit(solution)/shard_map/pallas_call | solution.py:685
  37.5 0.8 %shard_map.69 = (f32[512,128]{1,0:T(8,128)}, f32[512,128]{1,0:T(8,128)}) custom-call(f32[512,128]{1,0:T(8,128)S(1)} %get-tuple-element.6.sol_ref, f32[512,128]{1,0:T(8,128)S(1)} %get-tuple-element.7.res_ref), custom_call_target="tpu_custom_call" | custom-call | tf_op jit(solution)/shard_map/pallas_call | solution.py:753

commit v4 on v3

--- a/solution.py
+++ b/solution.py
@@ -440,6 +440,10 @@
         pltpu.make_async_copy(most, most, pr_sem.at[k]).wait()
         return jnp.sum(slots[k], axis=0)
 
+    def sum_sent(k):
+        most = slots.at[k, pl.ds(0, n - 1)]
+        pltpu.make_async_copy(most, most, ps_sem.at[k]).wait()
+
     def widened(v, size):
         return jnp.broadcast_to(v, (size, lanes))
 
@@ -580,9 +584,20 @@
                     x, y = corner_at(s, p, q)
                     wcsend[s - 4, pl.ds(i, 1), :] = wown[outer, pl.ds(x * b + y, 1), :]
             each((4, 5, 6, 7, 2, 3, 0, 1), lambda s: w_copy(s).start())
+            each(range(4), lambda s: all_do(
+                [image_copy(m, opposite[s]) for m in range(count)], "wait_recv"))
+            each(range(4, 8), lambda s: image_copy(0, opposite[s]).wait_recv())
         else:
             for x in range(a):
                 earlier(x)
+            for k in range(OUTER):
+                sum_sent(k)
+            each(range(8), lambda s: ground_copy(s).wait_send())
+            each(range(4), lambda s: all_do([field_copy(m, s) for m in range(nf)], "wait_send"))
+            each((0, 1, 4, 5, 6, 7), lambda s: all_do(deep_copies(s), "wait_send"))
+            each(range(8), lambda s: w_copy(s).wait_send())
+            each(range(4), lambda s: all_do([image_copy(m, s) for m in range(count)], "wait_send"))
+            each(range(4, 8), lambda s: image_copy(0, s).wait_send())
         row = sum_done(1 + outer)
 
         onto_row = jnp.where(lane8 < count, jnp.broadcast_to(row, (8, lanes)), 0.0)
@@ -622,9 +637,6 @@
             continue
         earlier = solution_update
 
-        for m in range(count):
-            each(range(4), lambda s: image_copy(m, opposite[s]).wait_recv())
-        each(range(4, 8), lambda s: image_copy(0, opposite[s]).wait_recv())
         each(range(8), lambda s: w_copy(opposite[s]).wait_recv())
         new = rwide.at[outer + 1]
         for side in range(2):
@@ -646,17 +658,7 @@
             ))
         along = along - step * (onto - times(gram, as_row(y)))
 
-    for k in range(OUTER + 1):
-        most = slots.at[k, pl.ds(0, n - 1)]
-        pltpu.make_async_copy(most, most, ps_sem.at[k]).wait()
-    each(range(8), lambda s: ground_copy(s).wait_send())
-    for m in range(nf):
-        each(range(4), lambda s: field_copy(m, s).wait_send())
-    each((0, 1, 4, 5, 6, 7), lambda s: all_do(deep_copies(s), "wait_send"))
-    each(range(8), lambda s: w_copy(s).wait_send())
-    for m in range(count):
-        each(range(4), lambda s: image_copy(m, s).wait_send())
-    each(range(4, 8), lambda s: image_copy(0, s).wait_send())
+    sum_sent(OUTER)
 
 
 def store(sol_ref, res_ref, sol_out, res_out, sem):

time: 38.6 us -> 38.4 us (level)
  no operation moved by 1% of the time
where the time goes in v4:
time: 38.4 us; the launch traced here: 38.2 us
  Pallas kernels  37.5 us (98%)
  between operations  0.64 us (2%)
    pallas_call x1, Pallas kernels, local(): pl.pallas_call(functools.partial(kernel, gxn, gyn, count, a, b), out_shap...  36.7 us
    pallas_call x1, Pallas kernels, local(): pl.pallas_call(store, out_shape=(field, field), in_specs=[vm] * 2, out_sp...  0.81 us

profile of v4, /device:TPU:0, one launch (start us, length us, event | category | flops | bytes accessed | tf_op | source)
XLA Modules:
  0.0 38.2 jit_solution(11144423252814549738)
XLA Ops:
  0.6 36.7 %shard_map.68 = (f32[512,128]{1,0:T(8,128)S(1)}, f32[512,128]{1,0:T(8,128)S(1)}) custom-call(f32[512,128]{1,0:T(8,128)} %bitcast.6, f32[512,128]{1,0:T(8,128)} %bitcast.7, bf16[8,512,128]{2,1,0:T(8,128)(2,1)} %bitcast.5, s32[16,32]{1,0:T(8,128)} %h_hbm.1, s32[16,32]{1,0:T(8,128)} %code_hbm.1), custom_call_target="tpu_custom_call" | custom-call | tf_op jit(solution)/shard_map/pallas_call | solution.py:687
  37.4 0.8 %shard_map.69 = (f32[512,128]{1,0:T(8,128)}, f32[512,128]{1,0:T(8,128)}) custom-call(f32[512,128]{1,0:T(8,128)S(1)} %get-tuple-element.6.sol_ref, f32[512,128]{1,0:T(8,128)S(1)} %get-tuple-element.7.res_ref), custom_call_target="tpu_custom_call" | custom-call | tf_op jit(solution)/shard_map/pallas_call | solution.py:755
